TPU v7x, 32 devices: a whole 2x2x4 slice. The times are simulated.
32 devices in a mesh: qrow: 8 (over z, x), kcol: 4 (over y, core).
Axes of the slice: x: 2, y: 2, z: 4, core: 2. Of those that a mesh axis runs over, the one named last changes fastest.
Arguments:
- queries: bfloat16 [128, 8192], P(('qrow', 'kcol')), may hold values from -200 to 200
- keys_values: bfloat16 [2, 4096, 512], P(None, ('kcol', 'qrow')), may hold values from -8 to 8
- doc_blocks: int32 [32], replicated, may hold values from 0 to 1, never falling along the last dimension, each value on 1 to 17 neighbouring positions
Outputs:
- attended: bfloat16 [128, 8192], P(('qrow', 'kcol'))
Inputs may be any that keep to these rules, and one draw needn't show every extreme that they name: doc_blocks[b] is the document of positions 128 b to 128 b + 127; each document covers 1 to 17 consecutive entries (blocks), one document exactly that many.
All inputs are finite; a program needn't handle non-finite values.
Results may differ from a plain program's by a relative error of at most 0.0046.
Values may be sent and summed in bfloat16 or wider, within the bound.
A program may use at most 128 MiB of HBM per device.

v0:
```python
import math

import jax
import jax.numpy as jnp
from jax import lax
from jax.experimental import pallas as pl
from jax.experimental.pallas import tpu as pltpu
from jax.sharding import PartitionSpec as P

QUERY_HEADS = 64
KEY_VALUE_HEADS = 4
HEAD_WIDTH = 128
BLOCK = 128
MESH = pl.DeviceIdType.MESH

masked_score = -1e30


def dot(a, b, dims):
    return lax.dot_general(a, b, (dims, ((), ())), preferred_element_type=jnp.float32)


def make_kernel(rows_n, cols_n, local_rows, blocks_n):
    fold = max(1, 8 // cols_n)
    groups = rows_n // fold
    members = fold * cols_n
    heads = QUERY_HEADS // members
    slice_rows = local_rows * heads
    chunk_rows = members * slice_rows
    devices = rows_n * cols_n
    total_queries = devices * local_rows
    query_blocks = total_queries // BLOCK
    stripe_blocks = blocks_n // query_blocks
    chunk_queries = members * local_rows
    assert BLOCK % chunk_queries == 0 and blocks_n == devices and cols_n % 2 == 0 and 2 * slice_rows <= BLOCK
    first_live = max(0, stripe_blocks - 1 - blocks_n // 2)
    block_of = lambda e, g: (e % cols_n) * rows_n + g * fold + e // cols_n
    spans = [[block_of(e, g) >= first_live for g in range(groups)] for e in range(members)]
    sure = [e for e in range(members) if all(spans[e])]
    maybe = [e for e in range(members) if any(spans[e]) and not all(spans[e])]
    slots = sure + maybe
    scale = math.log2(math.e) / math.sqrt(HEAD_WIDTH)

    apart = max(1, groups // 2)

    def visited(group, k):
        block = group // apart
        far = lax.rem(block + 1, groups // apart) * apart + lax.rem(group + k, apart)
        near = block * apart + lax.rem(group + k - apart, apart)
        return jnp.where(k == 0, group, jnp.where(k <= apart, far, near))

    def where_is(group, member):
        return (group * fold + member // cols_n, member % cols_n)

    def kernel(doc_ref, q_ref, kv_ref, out_ref, local, local_sem, qsend, wide, qbuf, kvbuf, osend, ssend, obuf, sbuf,
               q_send, q_recv, kv_send, kv_recv, pair_send, pair_recv, o_send, o_recv, s_send, s_recv):
        row, col = lax.axis_index("qrow"), lax.axis_index("kcol")
        group = row // fold
        member = (row % fold) * cols_n + col
        me = row * cols_n + col
        my_block = col * rows_n + row
        my_slot = sum(i * (member == e).astype(jnp.int32) for i, e in enumerate(slots))

        half = lax.rem(member, 2)
        barrier = pltpu.get_barrier_semaphore()

        fetch = pltpu.make_async_copy(kv_ref, local, local_sem)
        fetch.start()

        @pl.loop(1, devices)
        def _(k):
            other = lax.rem(me + k, devices)
            pl.semaphore_signal(barrier, inc=1, device_id=(other // cols_n, other % cols_n), device_id_type=MESH)

        for i, e in enumerate(maybe):
            @pl.when(block_of(e, group) < first_live)
            def _():
                kvbuf[:, len(sure) + i] = jnp.zeros((2, BLOCK, HEAD_WIDTH), kvbuf.dtype)

        for e in range(members):
            for h in range(heads):
                first = (e * heads + h) * HEAD_WIDTH
                wide[e, h * local_rows:(h + 1) * local_rows] = q_ref[:, first:first + HEAD_WIDTH].astype(jnp.float32)
            qsend[e] = wide[e].astype(qsend.dtype)

        fetch.wait()
        pl.semaphore_wait(barrier, devices - 1)

        def kv_part(e):
            first = pl.multiple_of(e * heads // (QUERY_HEADS // KEY_VALUE_HEADS) * HEAD_WIDTH, HEAD_WIDTH)
            return local.at[lax.rem(e, 2), :, pl.ds(first, HEAD_WIDTH)]

        def kv_copy(k):
            e = lax.rem(member + k, members)
            return pltpu.make_async_remote_copy(
                src_ref=kv_part(e), dst_ref=kvbuf.at[lax.rem(e, 2), my_slot], send_sem=kv_send.at[k],
                recv_sem=kv_recv.at[my_slot], device_id=where_is(group, e), device_id_type=MESH)

        @pl.when(my_block >= first_live)
        def _():
            pltpu.make_async_copy(kv_part(member), kvbuf.at[half, my_slot], kv_recv.at[my_slot]).start()
            for k in range(1, members):
                kv_copy(k).start()

        pltpu.make_async_copy(qsend.at[member], qbuf.at[me], q_recv.at[group]).start()

        @pl.loop(1, devices)
        def _(k):
            e = lax.rem(member + k, members)
            pltpu.make_async_remote_copy(
                src_ref=qsend.at[e], dst_ref=qbuf.at[me], send_sem=q_send, recv_sem=q_recv.at[group],
                device_id=where_is(visited(group, k // members), e), device_id_type=MESH).start()

        def pair_copy(i):
            return pltpu.make_async_remote_copy(
                src_ref=kvbuf.at[half, i], dst_ref=kvbuf.at[half, i], send_sem=pair_send.at[i],
                recv_sem=pair_recv.at[i], device_id=(row, col + 1 - 2 * lax.rem(col, 2)), device_id_type=MESH)

        def per_slot(step):
            for i, e in enumerate(slots):
                if e in sure:
                    step(i)
                else:
                    pl.when(block_of(e, group) >= first_live)(lambda: step(i))

        def pass_on(i):
            pltpu.make_async_copy(kvbuf.at[half, i], kvbuf.at[half, i], kv_recv.at[i]).wait()
            pair_copy(i).start()

        per_slot(pass_on)
        per_slot(lambda i: pair_copy(i).wait_recv())

        lane = lax.broadcasted_iota(jnp.int32, (chunk_rows, BLOCK), 1)
        row_index = lax.broadcasted_iota(jnp.int32, (chunk_rows, BLOCK), 0)
        row_query = row_index // slice_rows * local_rows + row_index % local_rows
        offset = (lax.broadcasted_iota(jnp.int32, (slice_rows, BLOCK), 1)
                  - lax.broadcasted_iota(jnp.int32, (slice_rows, BLOCK), 0))
        top_place, total_place = offset == 0, offset == slice_rows

        def attend(source):
            first = source * members
            mine = qbuf.at[pl.ds(first, members)]
            pltpu.make_async_copy(mine, mine, q_recv.at[source]).wait()
            q = qbuf[pl.ds(first, members)].reshape(chunk_rows, HEAD_WIDTH)
            query_first = source * chunk_queries
            query_block = (query_first // BLOCK + 1) * stripe_blocks - 1
            in_block = row_query + query_first % BLOCK
            query_doc = doc_ref[query_block]
            keys = kvbuf[0].reshape(len(slots) * BLOCK, HEAD_WIDTH)
            values = kvbuf[1].reshape(len(slots) * BLOCK, HEAD_WIDTH)
            scores = dot(q, keys, ((1,), (1,)))
            masked = []
            for i, e in enumerate(slots):
                b = block_of(e, group)
                same = doc_ref[b] == query_doc
                whole = jnp.where(same & (b < query_block), BLOCK, -1)
                causal = jnp.where(same & (b == query_block), 0, -2 * BLOCK)
                limit = jnp.maximum(in_block + causal, whole)
                masked.append(jnp.where(lane <= limit, scores[:, i * BLOCK:(i + 1) * BLOCK], masked_score))
            top = masked[0]
            for s in masked[1:]:
                top = jnp.maximum(top, s)
            top = jnp.maximum(jnp.max(top, axis=1, keepdims=True), 0.5 * masked_score)
            weights = [jnp.exp2((s - top) * scale) for s in masked]
            total = weights[0]
            for p in weights[1:]:
                total = total + p
            total = jnp.sum(total, axis=1, keepdims=True)
            acc = dot(jnp.concatenate([p.astype(jnp.bfloat16) for p in weights], axis=1), values, ((1,), (0,)))
            osend[pl.ds(first, members)] = acc.astype(jnp.bfloat16).reshape(members, slice_rows, HEAD_WIDTH)
            for j in range(members):
                part = slice(j * slice_rows, (j + 1) * slice_rows)
                stats = jnp.where(top_place, top[part], jnp.where(total_place, total[part], 0.0))
                ssend[first + j] = jnp.sum(stats, axis=0, keepdims=True)

        def give(source, j):
            k = source * members + j
            return [
                pltpu.make_async_remote_copy(
                    src_ref=src.at[k], dst_ref=dst.at[group, member], send_sem=sent, recv_sem=got.at[group],
                    device_id=where_is(source, j), device_id_type=MESH)
                for src, dst, sent, got in ((osend, obuf, o_send, o_recv), (ssend, sbuf, s_send, s_recv))
            ]

        def step(k):
            source = lax.rem(group + k, groups)
            attend(source)
            for j in range(members):
                for copy in give(source, j):
                    copy.start()

        if groups <= 4:
            for k in range(1, groups):
                step(k)
        else:
            pl.loop(1, groups)(step)

        attend(group)
        pltpu.make_async_copy(osend.at[me], obuf.at[group, member], o_recv.at[group]).start()
        pltpu.make_async_copy(ssend.at[me], sbuf.at[group, member], s_recv.at[group]).start()
        for i in range(1, members):
            for copy in give(group, lax.rem(member + i, members)):
                copy.start()

        for g in range(groups):
            pltpu.make_async_copy(sbuf.at[g], sbuf.at[g], s_recv.at[g]).wait()
            pltpu.make_async_copy(obuf.at[g], obuf.at[g], o_recv.at[g]).wait()

        for e in range(members):
            column = lambda g, place: jnp.sum(jnp.where(place, sbuf[g, e], 0.0), axis=1, keepdims=True)
            tops = [column(g, top_place) for g in range(groups)]
            overall = tops[0]
            for t in tops[1:]:
                overall = jnp.maximum(overall, t)
            merged = weight = None
            for g in range(groups):
                factor = jnp.exp2((tops[g] - overall) * scale)
                term = factor * obuf[g, e].astype(jnp.float32)
                part = factor * column(g, total_place)
                merged = term if merged is None else merged + term
                weight = part if weight is None else weight + part
            wide[e] = merged / weight
            for h in range(heads):
                first = (e * heads + h) * HEAD_WIDTH
                out_ref[:, first:first + HEAD_WIDTH] = wide[e, h * local_rows:(h + 1) * local_rows].astype(out_ref.dtype)

        per_slot(lambda i: pair_copy(i).wait_send())

        @pl.when(my_block >= first_live)
        def _():
            for k in range(1, members):
                kv_copy(k).wait_send()
        others = qbuf.at[pl.ds(0, devices - 1)]
        pltpu.make_async_copy(others, others, q_send).wait()
        others = osend.at[pl.ds(0, devices - 1)]
        pltpu.make_async_copy(others, others, o_send).wait()
        others = ssend.at[pl.ds(0, devices - 1)]
        pltpu.make_async_copy(others, others, s_send).wait()

    bf16, dma = jnp.bfloat16, pltpu.SemaphoreType.DMA
    scratch = [
        pltpu.VMEM((2, BLOCK, KEY_VALUE_HEADS * HEAD_WIDTH), bf16),
        dma,
        pltpu.VMEM((members, slice_rows, HEAD_WIDTH), bf16),
        pltpu.VMEM((members, slice_rows, HEAD_WIDTH), jnp.float32),
        pltpu.VMEM((devices, slice_rows, HEAD_WIDTH), bf16),
        pltpu.VMEM((2, len(slots), BLOCK, HEAD_WIDTH), bf16),
        pltpu.VMEM((devices, slice_rows, HEAD_WIDTH), bf16),
        pltpu.VMEM((devices, 1, BLOCK), jnp.float32),
        pltpu.VMEM((groups, members, slice_rows, HEAD_WIDTH), bf16),
        pltpu.VMEM((groups, members, 1, BLOCK), jnp.float32),
        dma, dma((groups,)), dma((members,)), dma((len(slots),)), dma((len(slots),)), dma((len(slots),)),
        dma, dma((groups,)), dma, dma((groups,)),
    ]
    return kernel, scratch


def solution(mesh):
    rows_n, cols_n = mesh.shape["qrow"], mesh.shape["kcol"]

    def per_device(queries, keys_values, doc_blocks):
        local_rows = queries.shape[0]
        kernel, scratch = make_kernel(rows_n, cols_n, queries.shape[0], doc_blocks.shape[0])
        return pl.pallas_call(
            kernel,
            out_shape=jax.ShapeDtypeStruct(queries.shape, queries.dtype),
            in_specs=[
                pl.BlockSpec(memory_space=pltpu.SMEM),
                pl.BlockSpec(memory_space=pltpu.VMEM),
                pl.BlockSpec(memory_space=pl.ANY),
            ],
            out_specs=pl.BlockSpec(memory_space=pltpu.VMEM),
            scratch_shapes=scratch,
            compiler_params=pltpu.CompilerParams(collective_id=0, has_side_effects=True),
        )(doc_blocks, queries, keys_values)

    return jax.shard_map(
        per_device,
        mesh=mesh,
        in_specs=(P(("qrow", "kcol"), None), P(None, ("kcol", "qrow"), None), P()),
        out_specs=P(("qrow", "kcol"), None),
        check_vma=False,
    )
```

profile of v0, /device:TPU:0, one launch (start us, length us, event | category | flops | bytes accessed | tf_op | source)
XLA Modules:
  0.0 24.6 jit_solution(2392125576509879503)
XLA Ops:
  0.0 23.1 %shard_map.37 = bf16[4,8192]{1,0:T(4,128)(2,1)} custom-call(s32[32]{0:T(128)} %doc_ref.1, bf16[4,8192]{1,0:T(4,128)(2,1)} %q_ref.1, bf16[2,128,512]{2,1,0:T(8,128)(2,1)} %kv_ref.1), custom_call_target="tpu_custom_call" | custom-call | tf_op jit(solution)/shard_map/pallas_call | solution.py:264
  23.2 1.5 %copy.5 = bf16[4,8192]{1,0:T(4,128)(2,1)} copy(bf16[4,8192]{1,0:T(4,128)(2,1)} %shard_map.37) | data formatting | bytes 131072
where the time goes:
time: 24.9 us; the launch traced here: 24.6 us
  Pallas kernels  23.1 us (93%)
  local copies, waits for them, and re-layouts  1.49 us (6%)
    pallas_call x1, Pallas kernels, per_device(): pl.pallas_call(kernel, out_shape=jax.ShapeDtypeStruct(queries.shape, quer...  23.1 us
    unnamed x1, local copies, waits for them, and re-layouts  1.49 us

commit v1 on v0

--- a/solution.py
+++ b/solution.py
@@ -52,7 +52,7 @@
     def where_is(group, member):
         return (group * fold + member // cols_n, member % cols_n)
 
-    def kernel(doc_ref, q_ref, kv_ref, out_ref, local, local_sem, qsend, wide, qbuf, kvbuf, osend, ssend, obuf, sbuf,
+    def kernel(doc_any, q_any, kv_ref, out_ref, doc_ref, q_ref, in_sems, local, local_sem, qsend, wide, qbuf, kvbuf, osend, ssend, obuf, sbuf,
                q_send, q_recv, kv_send, kv_recv, pair_send, pair_recv, o_send, o_recv, s_send, s_recv):
         row, col = lax.axis_index("qrow"), lax.axis_index("kcol")
         group = row // fold
@@ -64,19 +64,25 @@
         half = lax.rem(member, 2)
         barrier = pltpu.get_barrier_semaphore()
 
-        fetch = pltpu.make_async_copy(kv_ref, local, local_sem)
-        fetch.start()
-
         @pl.loop(1, devices)
         def _(k):
             other = lax.rem(me + k, devices)
             pl.semaphore_signal(barrier, inc=1, device_id=(other // cols_n, other % cols_n), device_id_type=MESH)
 
+        q_fetch = pltpu.make_async_copy(q_any, q_ref, in_sems.at[0])
+        q_fetch.start()
+        doc_fetch = pltpu.make_async_copy(doc_any, doc_ref, in_sems.at[1])
+        doc_fetch.start()
+        fetch = pltpu.make_async_copy(kv_ref, local, local_sem)
+        fetch.start()
+
         for i, e in enumerate(maybe):
             @pl.when(block_of(e, group) < first_live)
             def _():
                 kvbuf[:, len(sure) + i] = jnp.zeros((2, BLOCK, HEAD_WIDTH), kvbuf.dtype)
 
+        q_fetch.wait()
+        doc_fetch.wait()
         for e in range(members):
             for h in range(heads):
                 first = (e * heads + h) * HEAD_WIDTH
@@ -203,8 +209,8 @@
                 copy.start()
 
         for g in range(groups):
-            pltpu.make_async_copy(sbuf.at[g], sbuf.at[g], s_recv.at[g]).wait()
-            pltpu.make_async_copy(obuf.at[g], obuf.at[g], o_recv.at[g]).wait()
+          pltpu.make_async_copy(sbuf.at[g], sbuf.at[g], s_recv.at[g]).wait()
+          pltpu.make_async_copy(obuf.at[g], obuf.at[g], o_recv.at[g]).wait()
 
         for e in range(members):
             column = lambda g, place: jnp.sum(jnp.where(place, sbuf[g, e], 0.0), axis=1, keepdims=True)
@@ -239,6 +245,9 @@
 
     bf16, dma = jnp.bfloat16, pltpu.SemaphoreType.DMA
     scratch = [
+        pltpu.SMEM((blocks_n,), jnp.int32),
+        pltpu.VMEM((local_rows, QUERY_HEADS * HEAD_WIDTH), jnp.bfloat16),
+        pltpu.SemaphoreType.DMA((2,)),
         pltpu.VMEM((2, BLOCK, KEY_VALUE_HEADS * HEAD_WIDTH), bf16),
         dma,
         pltpu.VMEM((members, slice_rows, HEAD_WIDTH), bf16),
@@ -261,18 +270,20 @@
     def per_device(queries, keys_values, doc_blocks):
         local_rows = queries.shape[0]
         kernel, scratch = make_kernel(rows_n, cols_n, queries.shape[0], doc_blocks.shape[0])
-        return pl.pallas_call(
+        merged = pl.pallas_call(
             kernel,
-            out_shape=jax.ShapeDtypeStruct(queries.shape, queries.dtype),
+            out_shape=pltpu.VMEM(queries.shape, queries.dtype),
             in_specs=[
-                pl.BlockSpec(memory_space=pltpu.SMEM),
-                pl.BlockSpec(memory_space=pltpu.VMEM),
+                pl.BlockSpec(memory_space=pl.ANY),
+                pl.BlockSpec(memory_space=pl.ANY),
                 pl.BlockSpec(memory_space=pl.ANY),
             ],
             out_specs=pl.BlockSpec(memory_space=pltpu.VMEM),
             scratch_shapes=scratch,
             compiler_params=pltpu.CompilerParams(collective_id=0, has_side_effects=True),
         )(doc_blocks, queries, keys_values)
+
+        return merged
 
     return jax.shard_map(
         per_device,

time: 24.9 us -> 22.3 us (0.90)
  Pallas kernels: 23.1 us -> 21.5 us
  local copies, waits for them, and re-layouts: 1.49 us -> 0.63 us
    pallas_call x1, Pallas kernels: 23.1 us -> 21.5 us  [per_device(): pl.pallas_call(kernel, out_shape=pltpu.VMEM(queries.shape, queries.dtype)...]
    unnamed x1, local copies, waits for them, and re-layouts: 1.49 us -> 0.63 us
where the time goes in v1:
time: 22.3 us; the launch traced here: 22.2 us
  Pallas kernels  21.5 us (96%)
  local copies, waits for them, and re-layouts  0.63 us (3%)
    pallas_call x1, Pallas kernels, per_device(): pl.pallas_call(kernel, out_shape=pltpu.VMEM(queries.shape, queries.dtype)...  21.5 us
    unnamed x1, local copies, waits for them, and re-layouts  0.63 us

profile of v1, /device:TPU:0, one launch (start us, length us, event | category | flops | bytes accessed | tf_op | source)
XLA Modules:
  0.0 22.2 jit_solution(17922573736306174610)
XLA Ops:
  0.0 21.5 %shard_map.37 = bf16[4,8192]{1,0:T(4,128)(2,1)S(1)} custom-call(s32[32]{0:T(128)} %doc_any.1, bf16[4,8192]{1,0:T(4,128)(2,1)} %q_any.1, bf16[2,128,512]{2,1,0:T(8,128)(2,1)} %kv_ref.1), custom_call_target="tpu_custom_call" | custom-call | tf_op jit(solution)/shard_map/pallas_call | solution.py:273
  21.5 0.6 %copy.5 = bf16[4,8192]{1,0:T(4,128)(2,1)} copy(bf16[4,8192]{1,0:T(4,128)(2,1)S(1)} %shard_map.37) | data formatting | bytes 131072

commit v2 on v1

v2 whole, which is shorter than its diff:
```python
import math

import jax
import jax.numpy as jnp
from jax import lax
from jax.experimental import pallas as pl
from jax.experimental.pallas import tpu as pltpu
from jax.sharding import PartitionSpec as P

QUERY_HEADS = 64
KEY_VALUE_HEADS = 4
HEAD_WIDTH = 128
BLOCK = 128
MESH = pl.DeviceIdType.MESH

masked_score = -1e30


def dot(a, b, dims):
    return lax.dot_general(a, b, (dims, ((), ())), preferred_element_type=jnp.float32)


def make_kernel(rows_n, cols_n, local_rows, blocks_n):
    fold = max(1, 8 // cols_n)
    planes = rows_n // fold
    members = fold * cols_n
    chips = members // 2
    classes = planes // 2
    heads = QUERY_HEADS // members
    slice_rows = local_rows * heads
    chunk_rows = members * slice_rows
    devices = rows_n * cols_n
    total_queries = devices * local_rows
    query_blocks = total_queries // BLOCK
    stripe_blocks = blocks_n // query_blocks
    chunk_queries = members * local_rows
    messages = classes * members
    assert BLOCK % chunk_queries == 0 and blocks_n == devices and cols_n % 2 == 0 and 2 * slice_rows <= BLOCK
    assert planes % 2 == 0
    first_live = max(0, stripe_blocks - 1 - blocks_n // 2)
    block_of = lambda e, p: (e % cols_n) * rows_n + p * fold + e // cols_n
    alive = lambda e, half: [block_of(e, p) >= first_live for p in range(half, planes, 2)]
    sure = [e for e in range(members) if all(alive(e, 0) + alive(e, 1))]
    maybe = [(half, e) for half in range(2) for e in range(members) if e not in sure and any(alive(e, half))]
    spare = 2 * len(sure)
    slots_n = spare + len(maybe)
    scale = math.log2(math.e) / math.sqrt(HEAD_WIDTH)

    assert sure and chips & (chips - 1) == 0
    steps = sorted(range(1, chips), key=lambda k: (bin(k).count("1"), -k))

    def crossed(chip, k):
        bits = [1 << n for n in range(chips.bit_length() - 1) if k >> n & 1]
        return chip + sum(bit * (1 - 2 * (chip // bit % 2)) for bit in bits)

    def where_is(plane, member):
        return (plane * fold + member // cols_n, member % cols_n)

    def kernel(doc_any, q_any, kv_any, out_ref, doc_ref, q_ref, local, in_sems, plane_sem, cross_sem,
               qsend, wide, qbuf, kvbuf, early_top, early_total, early_acc, osend, ssend, obuf, sbuf,
               q_send, q_recv, kv_send, kv_recv, pass_send, relay_send, o_send, o_recv, s_send, s_recv):
        row, col = lax.axis_index("qrow"), lax.axis_index("kcol")
        plane, core = row // fold, lax.rem(col, 2)
        member = (row % fold) * cols_n + col
        chip = member // 2
        half, kind = lax.rem(plane, 2), plane // 2
        mate = plane + 1 - 2 * half
        me = kind * members + member
        my_block = block_of(member, plane)
        partner = (row, col + 1 - 2 * core)
        mate_core = where_is(mate, chip * 2 + 1)
        is_first, is_second = core == 0, core == 1
        barrier = pltpu.get_barrier_semaphore()

        def peer_plane(k):
            return lax.rem(kind + k, classes) * 2 + half

        def greet(plane_, member_):
            pl.semaphore_signal(barrier, inc=1, device_id=where_is(plane_, member_), device_id_type=MESH)

        for k in range(1, classes):
            for i in range(chips):
                greet(peer_plane(k), 2 * i + 1)
        greet(mate, chip * 2 + 1)
        for k in range(1, chips):
            greet(plane, lax.rem(chip + k, chips) * 2)
        pl.when(is_second)(lambda: greet(plane, chip * 2))

        fetch = pltpu.make_async_copy(kv_any, local, in_sems.at[1])
        fetch.start()
        q_fetch = pltpu.make_async_copy(q_any, q_ref, in_sems.at[0])
        q_fetch.start()
        doc_fetch = pltpu.make_async_copy(doc_any, doc_ref, in_sems.at[2])
        doc_fetch.start()

        for i, (h, e) in enumerate(maybe):
            @pl.when(block_of(e, 2 * kind + h) < first_live)
            def _():
                kvbuf[:, spare + i] = jnp.zeros((2, BLOCK, HEAD_WIDTH), kvbuf.dtype)

        @pl.when(is_first)
        def _():
            pl.semaphore_wait(barrier, members - 1)
            pl.semaphore_signal(plane_sem, inc=1, device_id=partner, device_id_type=MESH)

        @pl.when(is_second)
        def _():
            pl.semaphore_wait(plane_sem, 1)

        def remote(src, dst, sent, got, device):
            return pltpu.make_async_remote_copy(
                src_ref=src, dst_ref=dst, send_sem=sent, recv_sem=got, device_id=device, device_id_type=MESH)

        is_sure = sum((member == e).astype(jnp.int32) for e in sure)
        my_slot = sum(i * (member == e).astype(jnp.int32) for i, e in enumerate(sure))
        my_slot = my_slot + sum((spare + i) * ((member == e) & (half == h)).astype(jnp.int32)
                                for i, (h, e) in enumerate(maybe))
        my_slot_there = my_slot + len(sure) * is_sure

        def kv_part(c):
            first = pl.multiple_of(2 * c * heads // (QUERY_HEADS // KEY_VALUE_HEADS) * HEAD_WIDTH, HEAD_WIDTH)
            return local.at[:, :, pl.ds(first, HEAD_WIDTH)]

        def kv_copy(k):
            other = crossed(chip, k)
            return remote(kv_part(other), kvbuf.at[:, my_slot], kv_send.at[k], kv_recv.at[my_slot],
                          where_is(plane, other * 2 + 1))

        to_partner = remote(kv_part(chip), kvbuf.at[:, my_slot], kv_send.at[0], kv_recv.at[my_slot], partner)
        to_mate = remote(kv_part(chip), kvbuf.at[:, my_slot_there], kv_send.at[chips], kv_recv.at[my_slot_there],
                         mate_core)
        i_am_live = my_block >= first_live

        fetch.wait()

        @pl.when(i_am_live)
        def _():
            for k in steps:
                kv_copy(k).start()
            pltpu.make_async_copy(kv_part(chip), kvbuf.at[:, my_slot], kv_recv.at[my_slot]).start()
            to_partner.start()

        q_fetch.wait()
        for e in range(members):
            for h in range(heads):
                first = (e * heads + h) * HEAD_WIDTH
                wide[e, h * local_rows:(h + 1) * local_rows] = q_ref[:, first:first + HEAD_WIDTH].astype(jnp.float32)
            qsend[e] = wide[e].astype(qsend.dtype)
        doc_fetch.wait()

        def q_copy(k, j):
            e = lax.rem(member + j, members)
            return remote(qsend.at[e], qbuf.at[me], q_send, q_recv.at[kind], where_is(peer_plane(k), e))

        pltpu.make_async_copy(qsend.at[member], qbuf.at[me], q_recv.at[kind]).start()
        for j in range(1, members):
            q_copy(0, j).start()

        @pl.when(is_second)
        def _():
            pl.semaphore_wait(barrier, (classes - 1) * members + 2)
            pl.semaphore_signal(cross_sem, inc=1, device_id=partner, device_id_type=MESH)

        @pl.when(is_first)
        def _():
            pl.semaphore_wait(cross_sem, 1)

        pl.when(i_am_live)(to_mate.start)
        for k in range(1, classes):
            for j in range(members):
                q_copy(k, j).start()

        def landed(i):
            pltpu.make_async_copy(kvbuf.at[:, i], kvbuf.at[:, i], kv_recv.at[i]).wait()

        def to_first(i):
            return remote(kvbuf.at[:, i], kvbuf.at[:, i], pass_send.at[i], kv_recv.at[i], partner)

        def to_next(i, there):
            return remote(kvbuf.at[:, i], kvbuf.at[:, there], relay_send.at[i], kv_recv.at[there], mate_core)

        def in_order(of_half, first, step):
            for i, (h, e) in enumerate(maybe):
                is_live = (of_half == h) & (block_of(e, 2 * kind + h) >= first_live)
                pl.when(is_live)(lambda: step(spare + i, spare + i, e))
            for k in [0] + steps:
                for c in (1, 0):
                    e = crossed(chip, k) * 2 + c
                    i = sum(n * (e == f).astype(jnp.int32) for n, f in enumerate(sure))
                    found = sum((e == f).astype(jnp.int32) for f in sure) == 1
                    pl.when(found)(lambda: step(first + i, len(sure) + i, e))

        def own_slots(step):
            in_order(half, 0, step)

        def mate_slots(step):
            in_order(1 - half, len(sure), step)

        def hand_on(i, there, e):
            landed(i)

            @pl.when(is_second & (chip != e // 2))
            def _():
                to_next(i, there).start()
                to_first(i).start()

        def hand_over(i, there, e):
            landed(i)
            pl.when(is_second)(to_first(i).start)

        own_slots(hand_on)

        lane = lax.broadcasted_iota(jnp.int32, (chunk_rows, BLOCK), 1)
        row_index = lax.broadcasted_iota(jnp.int32, (chunk_rows, BLOCK), 0)
        row_query = row_index // slice_rows * local_rows + row_index % local_rows
        offset = (lax.broadcasted_iota(jnp.int32, (slice_rows, BLOCK), 1)
                  - lax.broadcasted_iota(jnp.int32, (slice_rows, BLOCK), 0))
        top_place, total_place = offset == 0, offset == slice_rows

        def part_of(source, members_part, first_slot, blocks):
            first, count = source // 2 * members + members_part.start, members_part.stop - members_part.start
            rows = slice(members_part.start * slice_rows, members_part.stop * slice_rows)
            q = qbuf[pl.ds(first, count)].reshape(count * slice_rows, HEAD_WIDTH)
            query_first = source * chunk_queries
            query_block = (query_first // BLOCK + 1) * stripe_blocks - 1
            in_block = row_query[rows] + query_first % BLOCK
            query_doc = doc_ref[query_block]
            held = slice(first_slot, first_slot + len(blocks))
            keys = kvbuf[0, held].reshape(len(blocks) * BLOCK, HEAD_WIDTH)
            values = kvbuf[1, held].reshape(len(blocks) * BLOCK, HEAD_WIDTH)
            scores = dot(q, keys, ((1,), (1,)))
            masked = []
            for i, b in enumerate(blocks):
                same = doc_ref[b] == query_doc
                whole = jnp.where(same & (b < query_block), BLOCK, -1)
                causal = jnp.where(same & (b == query_block), 0, -2 * BLOCK)
                limit = jnp.maximum(in_block + causal, whole)
                masked.append(jnp.where(lane[rows] <= limit, scores[:, i * BLOCK:(i + 1) * BLOCK], masked_score))
            top = masked[0]
            for s in masked[1:]:
                top = jnp.maximum(top, s)
            top = jnp.maximum(jnp.max(top, axis=1, keepdims=True), 0.5 * masked_score)
            weights = [jnp.exp2((s - top) * scale) for s in masked]
            total = weights[0]
            for p in weights[1:]:
                total = total + p
            total = jnp.sum(total, axis=1, keepdims=True)
            acc = dot(jnp.concatenate([p.astype(jnp.bfloat16) for p in weights], axis=1), values, ((1,), (0,)))
            return top, total, acc

        own_blocks = [block_of(e, plane) for e in sure]
        late_blocks = [block_of(e, mate) for e in sure] + [block_of(e, 2 * kind + h) for h, e in maybe]
        everyone = slice(0, members)
        pieces = [slice(0, members // 2), slice(members // 2, members)]

        def begin(source):
            mine = qbuf.at[pl.ds(source // 2 * members, members)]
            pltpu.make_async_copy(mine, mine, q_recv.at[source // 2]).wait()
            top, total, acc = part_of(source, everyone, 0, own_blocks)
            early_acc[source // 2] = acc
            early_top[source // 2] = jnp.broadcast_to(top, (chunk_rows, HEAD_WIDTH))
            early_total[source // 2] = jnp.broadcast_to(total, (chunk_rows, HEAD_WIDTH))

        def joined(parts):
            overall = parts[0][0]
            for part in parts[1:]:
                overall = jnp.maximum(overall, part[0])
            factors = [jnp.exp2((part[0] - overall) * scale) for part in parts]
            total = sum(f * part[1] for f, part in zip(factors, parts))
            acc = sum(f * part[2] for f, part in zip(factors, parts))
            return overall, total, acc

        def finish(source, members_part):
            rows = slice(members_part.start * slice_rows, members_part.stop * slice_rows)
            first, count = source // 2 * members + members_part.start, members_part.stop - members_part.start
            early = [ref[source // 2, rows] for ref in (early_top, early_total, early_acc)]
            top, total, acc = joined([early, part_of(source, members_part, len(sure), late_blocks)])
            osend[pl.ds(first, count)] = acc.astype(jnp.bfloat16).reshape(count, slice_rows, HEAD_WIDTH)
            for j in range(count):
                part = slice(j * slice_rows, (j + 1) * slice_rows)
                stats = jnp.where(top_place, top[part], jnp.where(total_place, total[part], 0.0))
                ssend[first + j] = jnp.sum(stats, axis=0, keepdims=True)

        def give(source, j):
            k = source // 2 * members + j
            device = where_is(source, j)
            return [remote(osend.at[k], obuf.at[kind, member], o_send, o_recv.at[kind], device),
                    remote(ssend.at[k], sbuf.at[kind, member], s_send, s_recv.at[kind], device)]

        begin(plane)
        for k in range(1, classes):
            begin(peer_plane(k))

        mate_slots(hand_over)

        for k in range(1, classes):
            for piece in pieces:
                finish(peer_plane(k), piece)
                for j in range(piece.start, piece.stop):
                    for copy in give(peer_plane(k), j):
                        copy.start()

        finish(plane, everyone)
        pltpu.make_async_copy(osend.at[me], obuf.at[kind, member], o_recv.at[kind]).start()
        pltpu.make_async_copy(ssend.at[me], sbuf.at[kind, member], s_recv.at[kind]).start()
        for i in range(1, members):
            for copy in give(plane, lax.rem(member + i, members)):
                copy.start()

        for g in range(classes):
            pltpu.make_async_copy(sbuf.at[g], sbuf.at[g], s_recv.at[g]).wait()
            pltpu.make_async_copy(obuf.at[g], obuf.at[g], o_recv.at[g]).wait()

        for e in range(members):
            column = lambda g, place: jnp.sum(jnp.where(place, sbuf[g, e], 0.0), axis=1, keepdims=True)
            tops = [column(g, top_place) for g in range(classes)]
            overall = tops[0]
            for t in tops[1:]:
                overall = jnp.maximum(overall, t)
            merged = weight = None
            for g in range(classes):
                factor = jnp.exp2((tops[g] - overall) * scale)
                term = factor * obuf[g, e].astype(jnp.float32)
                part = factor * column(g, total_place)
                merged = term if merged is None else merged + term
                weight = part if weight is None else weight + part
            wide[e] = merged / weight
            for h in range(heads):
                first = (e * heads + h) * HEAD_WIDTH
                out_ref[:, first:first + HEAD_WIDTH] = wide[e, h * local_rows:(h + 1) * local_rows].astype(out_ref.dtype)

        @pl.when(i_am_live)
        def _():
            to_partner.wait_send()
            for k in range(1, chips):
                kv_copy(k).wait_send()
            to_mate.wait_send()

        def own_sent(i, there, e):
            @pl.when(is_second & (chip != e // 2))
            def _():
                to_next(i, there).wait_send()
                to_first(i).wait_send()

        own_slots(own_sent)
        mate_slots(lambda i, there, e: pl.when(is_second)(to_first(i).wait_send))
        for buffer, sem in ((qbuf, q_send), (osend, o_send), (ssend, s_send)):
            others = buffer.at[pl.ds(0, messages - 1)]
            pltpu.make_async_copy(others, others, sem).wait()

    bf16, dma = jnp.bfloat16, pltpu.SemaphoreType.DMA
    signal = pltpu.SemaphoreType.REGULAR
    scratch = [
        pltpu.SMEM((blocks_n,), jnp.int32),
        pltpu.VMEM((local_rows, QUERY_HEADS * HEAD_WIDTH), bf16),
        pltpu.VMEM((2, BLOCK, KEY_VALUE_HEADS * HEAD_WIDTH), bf16),
        dma((3,)), signal, signal,
        pltpu.VMEM((members, slice_rows, HEAD_WIDTH), bf16),
        pltpu.VMEM((members, slice_rows, HEAD_WIDTH), jnp.float32),
        pltpu.VMEM((messages, slice_rows, HEAD_WIDTH), bf16),
        pltpu.VMEM((2, slots_n, BLOCK, HEAD_WIDTH), bf16),
        pltpu.VMEM((classes, chunk_rows, HEAD_WIDTH), jnp.float32),
        pltpu.VMEM((classes, chunk_rows, HEAD_WIDTH), jnp.float32),
        pltpu.VMEM((classes, chunk_rows, HEAD_WIDTH), jnp.float32),
        pltpu.VMEM((messages, slice_rows, HEAD_WIDTH), bf16),
        pltpu.VMEM((messages, 1, BLOCK), jnp.float32),
        pltpu.VMEM((classes, members, slice_rows, HEAD_WIDTH), bf16),
        pltpu.VMEM((classes, members, 1, BLOCK), jnp.float32),
        dma, dma((classes,)), dma((chips + 1,)), dma((slots_n,)), dma((slots_n,)), dma((slots_n,)),
        dma, dma((classes,)), dma, dma((classes,)),
    ]
    return kernel, scratch


def solution(mesh):
    rows_n, cols_n = mesh.shape["qrow"], mesh.shape["kcol"]

    def per_device(queries, keys_values, doc_blocks):
        local_rows = queries.shape[0]
        kernel, scratch = make_kernel(rows_n, cols_n, queries.shape[0], doc_blocks.shape[0])
        merged = pl.pallas_call(
            kernel,
            out_shape=pltpu.VMEM(queries.shape, queries.dtype),
            in_specs=[
                pl.BlockSpec(memory_space=pl.ANY),
                pl.BlockSpec(memory_space=pl.ANY),
                pl.BlockSpec(memory_space=pl.ANY),
            ],
            out_specs=pl.BlockSpec(memory_space=pltpu.VMEM),
            scratch_shapes=scratch,
            compiler_params=pltpu.CompilerParams(collective_id=0, has_side_effects=True),
        )(doc_blocks, queries, keys_values)

        return merged

    return jax.shard_map(
        per_device,
        mesh=mesh,
        in_specs=(P(("qrow", "kcol"), None), P(None, ("kcol", "qrow"), None), P()),
        out_specs=P(("qrow", "kcol"), None),
        check_vma=False,
    )
```

time: 22.3 us -> 21.9 us (0.982)
  Pallas kernels: 21.5 us -> 21.2 us
    pallas_call x1, Pallas kernels: 21.5 us -> 21.2 us  [per_device(): pl.pallas_call(kernel, out_shape=pltpu.VMEM(queries.shape, queries.dtype)...]
where the time goes in v2:
time: 21.9 us; the launch traced here: 21.8 us
  Pallas kernels  21.2 us (97%)
  local copies, waits for them, and re-layouts  0.63 us (3%)
    pallas_call x1, Pallas kernels, per_device(): pl.pallas_call(kernel, out_shape=pltpu.VMEM(queries.shape, queries.dtype)...  21.2 us
    unnamed x1, local copies, waits for them, and re-layouts  0.63 us

profile of v2, /device:TPU:0, one launch (start us, length us, event | category | flops | bytes accessed | tf_op | source)
XLA Modules:
  0.0 21.8 jit_solution(575495129444902730)
XLA Ops:
  0.0 21.2 %shard_map.37 = bf16[4,8192]{1,0:T(4,128)(2,1)S(1)} custom-call(s32[32]{0:T(128)} %doc_any.1, bf16[4,8192]{1,0:T(4,128)(2,1)} %q_any.1, bf16[2,128,512]{2,1,0:T(8,128)(2,1)} %kv_any.1), custom_call_target="tpu_custom_call" | custom-call | tf_op jit(solution)/shard_map/pallas_call | solution.py:381
  21.2 0.6 %copy.5 = bf16[4,8192]{1,0:T(4,128)(2,1)} copy(bf16[4,8192]{1,0:T(4,128)(2,1)S(1)} %shard_map.37) | data formatting | bytes 131072

commit v3 on v2

--- a/solution.py
+++ b/solution.py
@@ -78,13 +78,13 @@
         def greet(plane_, member_):
             pl.semaphore_signal(barrier, inc=1, device_id=where_is(plane_, member_), device_id_type=MESH)
 
+        for k in range(1, chips):
+            greet(plane, lax.rem(chip + k, chips) * 2 + 1)
+        pl.when(is_first)(lambda: greet(plane, chip * 2 + 1))
         for k in range(1, classes):
             for i in range(chips):
-                greet(peer_plane(k), 2 * i + 1)
-        greet(mate, chip * 2 + 1)
-        for k in range(1, chips):
-            greet(plane, lax.rem(chip + k, chips) * 2)
-        pl.when(is_second)(lambda: greet(plane, chip * 2))
+                greet(peer_plane(k), 2 * i)
+        greet(mate, chip * 2)
 
         fetch = pltpu.make_async_copy(kv_any, local, in_sems.at[1])
         fetch.start()
@@ -98,12 +98,12 @@
             def _():
                 kvbuf[:, spare + i] = jnp.zeros((2, BLOCK, HEAD_WIDTH), kvbuf.dtype)
 
-        @pl.when(is_first)
+        @pl.when(is_second)
         def _():
             pl.semaphore_wait(barrier, members - 1)
             pl.semaphore_signal(plane_sem, inc=1, device_id=partner, device_id_type=MESH)
 
-        @pl.when(is_second)
+        @pl.when(is_first)
         def _():
             pl.semaphore_wait(plane_sem, 1)
 
@@ -156,12 +156,12 @@
         for j in range(1, members):
             q_copy(0, j).start()
 
-        @pl.when(is_second)
+        @pl.when(is_first)
         def _():
             pl.semaphore_wait(barrier, (classes - 1) * members + 2)
             pl.semaphore_signal(cross_sem, inc=1, device_id=partner, device_id_type=MESH)
 
-        @pl.when(is_first)
+        @pl.when(is_second)
         def _():
             pl.semaphore_wait(cross_sem, 1)
 
@@ -180,15 +180,16 @@
             return remote(kvbuf.at[:, i], kvbuf.at[:, there], relay_send.at[i], kv_recv.at[there], mate_core)
 
         def in_order(of_half, first, step):
-            for i, (h, e) in enumerate(maybe):
-                is_live = (of_half == h) & (block_of(e, 2 * kind + h) >= first_live)
-                pl.when(is_live)(lambda: step(spare + i, spare + i, e))
             for k in [0] + steps:
                 for c in (1, 0):
                     e = crossed(chip, k) * 2 + c
                     i = sum(n * (e == f).astype(jnp.int32) for n, f in enumerate(sure))
                     found = sum((e == f).astype(jnp.int32) for f in sure) == 1
                     pl.when(found)(lambda: step(first + i, len(sure) + i, e))
+                    for n, (h, f) in enumerate(maybe):
+                        if f % 2 == c:
+                            is_live = (e == f) & (of_half == h) & (block_of(f, 2 * kind + h) >= first_live)
+                            pl.when(is_live)(lambda: step(spare + n, spare + n, f))
 
         def own_slots(step):
             in_order(half, 0, step)

time: 21.9 us -> 20.8 us (0.950)
  Pallas kernels: 21.2 us -> 20.1 us
    pallas_call x1, Pallas kernels: 21.2 us -> 20.1 us  [per_device(): pl.pallas_call(kernel, out_shape=pltpu.VMEM(queries.shape, queries.dtype)...]
where the time goes in v3:
time: 20.8 us; the launch traced here: 20.7 us
  Pallas kernels  20.1 us (97%)
  local copies, waits for them, and re-layouts  0.63 us (3%)
    pallas_call x1, Pallas kernels, per_device(): pl.pallas_call(kernel, out_shape=pltpu.VMEM(queries.shape, queries.dtype)...  20.1 us
    unnamed x1, local copies, waits for them, and re-layouts  0.63 us

profile of v3, /device:TPU:0, one launch (start us, length us, event | category | flops | bytes accessed | tf_op | source)
XLA Modules:
  0.0 20.7 jit_solution(629146928868855085)
XLA Ops:
  0.0 20.1 %shard_map.37 = bf16[4,8192]{1,0:T(4,128)(2,1)S(1)} custom-call(s32[32]{0:T(128)} %doc_any.1, bf16[4,8192]{1,0:T(4,128)(2,1)} %q_any.1, bf16[2,128,512]{2,1,0:T(8,128)(2,1)} %kv_any.1), custom_call_target="tpu_custom_call" | custom-call | tf_op jit(solution)/shard_map/pallas_call | solution.py:382
  20.1 0.6 %copy.5 = bf16[4,8192]{1,0:T(4,128)(2,1)} copy(bf16[4,8192]{1,0:T(4,128)(2,1)S(1)} %shard_map.37) | data formatting | bytes 131072

commit v4 on v3

--- a/solution.py
+++ b/solution.py
@@ -46,6 +46,7 @@
     slots_n = spare + len(maybe)
     scale = math.log2(math.e) / math.sqrt(HEAD_WIDTH)
 
+    assert chips + 1 <= slots_n
     assert sure and chips & (chips - 1) == 0
     steps = sorted(range(1, chips), key=lambda k: (bin(k).count("1"), -k))
 
@@ -56,9 +57,9 @@
     def where_is(plane, member):
         return (plane * fold + member // cols_n, member % cols_n)
 
-    def kernel(doc_any, q_any, kv_any, out_ref, doc_ref, q_ref, local, in_sems, plane_sem, cross_sem,
-               qsend, wide, qbuf, kvbuf, early_top, early_total, early_acc, osend, ssend, obuf, sbuf,
-               q_send, q_recv, kv_send, kv_recv, pass_send, relay_send, o_send, o_recv, s_send, s_recv):
+    def kernel(doc_any, q_any, kv_any, out_ref, doc_ref, q_ref, local, plane_sem, cross_sem,
+               qsend, wide, qbuf, kvbuf, early_top, early_total, early_acc, late_top, late_total, late_weights, osend, ssend, obuf, sbuf,
+               q_send, q_recv, kv_send, kv_recv, pass_send, o_send, o_recv, s_send, s_recv):
         row, col = lax.axis_index("qrow"), lax.axis_index("kcol")
         plane, core = row // fold, lax.rem(col, 2)
         member = (row % fold) * cols_n + col
@@ -71,6 +72,8 @@
         mate_core = where_is(mate, chip * 2 + 1)
         is_first, is_second = core == 0, core == 1
         barrier = pltpu.get_barrier_semaphore()
+        fetch = pltpu.make_async_copy(kv_any, local, kv_send)
+        fetch.start()
 
         def peer_plane(k):
             return lax.rem(kind + k, classes) * 2 + half
@@ -86,11 +89,9 @@
                 greet(peer_plane(k), 2 * i)
         greet(mate, chip * 2)
 
-        fetch = pltpu.make_async_copy(kv_any, local, in_sems.at[1])
-        fetch.start()
-        q_fetch = pltpu.make_async_copy(q_any, q_ref, in_sems.at[0])
+        q_fetch = pltpu.make_async_copy(q_any, q_ref, q_send)
         q_fetch.start()
-        doc_fetch = pltpu.make_async_copy(doc_any, doc_ref, in_sems.at[2])
+        doc_fetch = pltpu.make_async_copy(doc_any, doc_ref, o_send)
         doc_fetch.start()
 
         for i, (h, e) in enumerate(maybe):
@@ -117,28 +118,34 @@
                                 for i, (h, e) in enumerate(maybe))
         my_slot_there = my_slot + len(sure) * is_sure
 
-        def kv_part(c):
+        def kv_part(t, c):
             first = pl.multiple_of(2 * c * heads // (QUERY_HEADS // KEY_VALUE_HEADS) * HEAD_WIDTH, HEAD_WIDTH)
-            return local.at[:, :, pl.ds(first, HEAD_WIDTH)]
-
-        def kv_copy(k):
+            return local.at[t, :, pl.ds(first, HEAD_WIDTH)]
+
+        def kv_copy(t, k):
             other = crossed(chip, k)
-            return remote(kv_part(other), kvbuf.at[:, my_slot], kv_send.at[k], kv_recv.at[my_slot],
+            return remote(kv_part(t, other), kvbuf.at[t, my_slot], kv_send, kv_recv.at[t, my_slot],
                           where_is(plane, other * 2 + 1))
 
-        to_partner = remote(kv_part(chip), kvbuf.at[:, my_slot], kv_send.at[0], kv_recv.at[my_slot], partner)
-        to_mate = remote(kv_part(chip), kvbuf.at[:, my_slot_there], kv_send.at[chips], kv_recv.at[my_slot_there],
-                         mate_core)
+        def to_partner(t):
+            return remote(kv_part(t, chip), kvbuf.at[t, my_slot], kv_send, kv_recv.at[t, my_slot], partner)
+
+        def to_mate(t):
+            return remote(kv_part(t, chip), kvbuf.at[t, my_slot_there], kv_send,
+                          kv_recv.at[t, my_slot_there], mate_core)
+
         i_am_live = my_block >= first_live
 
         fetch.wait()
 
         @pl.when(i_am_live)
         def _():
-            for k in steps:
-                kv_copy(k).start()
-            pltpu.make_async_copy(kv_part(chip), kvbuf.at[:, my_slot], kv_recv.at[my_slot]).start()
-            to_partner.start()
+            for t in range(2):
+                for k in steps:
+                    kv_copy(t, k).start()
+            for t in range(2):
+                pltpu.make_async_copy(kv_part(t, chip), kvbuf.at[t, my_slot], kv_recv.at[t, my_slot]).start()
+                to_partner(t).start()
 
         q_fetch.wait()
         for e in range(members):
@@ -148,13 +155,27 @@
             qsend[e] = wide[e].astype(qsend.dtype)
         doc_fetch.wait()
 
-        def q_copy(k, j):
-            e = lax.rem(member + j, members)
+        def q_copy(k, e):
             return remote(qsend.at[e], qbuf.at[me], q_send, q_recv.at[kind], where_is(peer_plane(k), e))
 
+        def q_to(k, chips_crossed):
+            for n in chips_crossed:
+                for c in range(2):
+                    if n == 0 and k == 0:
+                        if c == 0:
+                            q_copy(0, member + 1 - 2 * core).start()
+                    else:
+                        q_copy(k, crossed(chip, n) * 2 + c).start()
+
+        near = [n for n in range(chips) if n % 2 == 0]
+        far = [n for n in range(chips) if n % 2 == 1]
+
+        def q_far():
+            for k in range(classes):
+                q_to(k, far)
+
         pltpu.make_async_copy(qsend.at[member], qbuf.at[me], q_recv.at[kind]).start()
-        for j in range(1, members):
-            q_copy(0, j).start()
+        q_to(0, near)
 
         @pl.when(is_first)
         def _():
@@ -165,19 +186,23 @@
         def _():
             pl.semaphore_wait(cross_sem, 1)
 
-        pl.when(i_am_live)(to_mate.start)
+        @pl.when(i_am_live)
+        def _():
+            to_mate(0).start()
+            to_mate(1).start()
+
         for k in range(1, classes):
-            for j in range(members):
-                q_copy(k, j).start()
-
-        def landed(i):
-            pltpu.make_async_copy(kvbuf.at[:, i], kvbuf.at[:, i], kv_recv.at[i]).wait()
-
-        def to_first(i):
-            return remote(kvbuf.at[:, i], kvbuf.at[:, i], pass_send.at[i], kv_recv.at[i], partner)
-
-        def to_next(i, there):
-            return remote(kvbuf.at[:, i], kvbuf.at[:, there], relay_send.at[i], kv_recv.at[there], mate_core)
+            q_to(k, near)
+        q_far()
+
+        def landed(t, i):
+            pltpu.make_async_copy(kvbuf.at[t, i], kvbuf.at[t, i], kv_recv.at[t, i]).wait()
+
+        def to_first(t, i):
+            return remote(kvbuf.at[t, i], kvbuf.at[t, i], pass_send.at[i], kv_recv.at[t, i], partner)
+
+        def to_next(t, i, there):
+            return remote(kvbuf.at[t, i], kvbuf.at[t, there], pass_send.at[i], kv_recv.at[t, there], mate_core)
 
         def in_order(of_half, first, step):
             for k in [0] + steps:
@@ -197,19 +222,24 @@
         def mate_slots(step):
             in_order(1 - half, len(sure), step)
 
-        def hand_on(i, there, e):
-            landed(i)
-
-            @pl.when(is_second & (chip != e // 2))
-            def _():
-                to_next(i, there).start()
-                to_first(i).start()
-
-        def hand_over(i, there, e):
-            landed(i)
-            pl.when(is_second)(to_first(i).start)
-
-        own_slots(hand_on)
+        def hand_on(t):
+            def step(i, there, e):
+                landed(t, i)
+
+                @pl.when(is_second & (chip != e // 2))
+                def _():
+                    to_next(t, i, there).start()
+                    to_first(t, i).start()
+            return step
+
+        def hand_over(t):
+            def step(i, there, e):
+                landed(t, i)
+                to_first(t, i).start()
+            return step
+
+        own_slots(hand_on(0))
+        own_slots(hand_on(1))
 
         lane = lax.broadcasted_iota(jnp.int32, (chunk_rows, BLOCK), 1)
         row_index = lax.broadcasted_iota(jnp.int32, (chunk_rows, BLOCK), 0)
@@ -218,17 +248,16 @@
                   - lax.broadcasted_iota(jnp.int32, (slice_rows, BLOCK), 0))
         top_place, total_place = offset == 0, offset == slice_rows
 
-        def part_of(source, members_part, first_slot, blocks):
-            first, count = source // 2 * members + members_part.start, members_part.stop - members_part.start
+        def weigh(k, members_part, first_slot, blocks):
+            first, count = k * members + members_part.start, members_part.stop - members_part.start
             rows = slice(members_part.start * slice_rows, members_part.stop * slice_rows)
             q = qbuf[pl.ds(first, count)].reshape(count * slice_rows, HEAD_WIDTH)
-            query_first = source * chunk_queries
+            query_first = (2 * k + half) * chunk_queries
             query_block = (query_first // BLOCK + 1) * stripe_blocks - 1
             in_block = row_query[rows] + query_first % BLOCK
             query_doc = doc_ref[query_block]
             held = slice(first_slot, first_slot + len(blocks))
             keys = kvbuf[0, held].reshape(len(blocks) * BLOCK, HEAD_WIDTH)
-            values = kvbuf[1, held].reshape(len(blocks) * BLOCK, HEAD_WIDTH)
             scores = dot(q, keys, ((1,), (1,)))
             masked = []
             for i, b in enumerate(blocks):
@@ -246,21 +275,32 @@
             for p in weights[1:]:
                 total = total + p
             total = jnp.sum(total, axis=1, keepdims=True)
-            acc = dot(jnp.concatenate([p.astype(jnp.bfloat16) for p in weights], axis=1), values, ((1,), (0,)))
-            return top, total, acc
+            return top, total, jnp.concatenate([p.astype(jnp.bfloat16) for p in weights], axis=1)
+
+        def summed(weights, first_slot):
+            count = weights.shape[1] // BLOCK
+            values = kvbuf[1, first_slot:first_slot + count].reshape(count * BLOCK, HEAD_WIDTH)
+            return dot(weights, values, ((1,), (0,)))
+
+        def part_of(k, members_part, first_slot, blocks):
+            top, total, weights = weigh(k, members_part, first_slot, blocks)
+            return top, total, summed(weights, first_slot)
 
         own_blocks = [block_of(e, plane) for e in sure]
         late_blocks = [block_of(e, mate) for e in sure] + [block_of(e, 2 * kind + h) for h, e in maybe]
         everyone = slice(0, members)
         pieces = [slice(0, members // 2), slice(members // 2, members)]
 
-        def begin(source):
-            mine = qbuf.at[pl.ds(source // 2 * members, members)]
-            pltpu.make_async_copy(mine, mine, q_recv.at[source // 2]).wait()
-            top, total, acc = part_of(source, everyone, 0, own_blocks)
-            early_acc[source // 2] = acc
-            early_top[source // 2] = jnp.broadcast_to(top, (chunk_rows, HEAD_WIDTH))
-            early_total[source // 2] = jnp.broadcast_to(total, (chunk_rows, HEAD_WIDTH))
+        def await_queries(k):
+            mine = qbuf.at[pl.ds(k * members, members)]
+            pltpu.make_async_copy(mine, mine, q_recv.at[k]).wait()
+
+        def begin(k):
+            await_queries(k)
+            top, total, acc = part_of(k, everyone, 0, own_blocks)
+            early_acc[...] = acc
+            early_top[...] = jnp.broadcast_to(top, (chunk_rows, HEAD_WIDTH))
+            early_total[...] = jnp.broadcast_to(total, (chunk_rows, HEAD_WIDTH))
 
         def joined(parts):
             overall = parts[0][0]
@@ -271,46 +311,97 @@
             acc = sum(f * part[2] for f, part in zip(factors, parts))
             return overall, total, acc
 
-        def finish(source, members_part):
-            rows = slice(members_part.start * slice_rows, members_part.stop * slice_rows)
-            first, count = source // 2 * members + members_part.start, members_part.stop - members_part.start
-            early = [ref[source // 2, rows] for ref in (early_top, early_total, early_acc)]
-            top, total, acc = joined([early, part_of(source, members_part, len(sure), late_blocks)])
+        def put(k, members_part, top, total, acc):
+            first, count = k * members + members_part.start, members_part.stop - members_part.start
             osend[pl.ds(first, count)] = acc.astype(jnp.bfloat16).reshape(count, slice_rows, HEAD_WIDTH)
             for j in range(count):
                 part = slice(j * slice_rows, (j + 1) * slice_rows)
                 stats = jnp.where(top_place, top[part], jnp.where(total_place, total[part], 0.0))
                 ssend[first + j] = jnp.sum(stats, axis=0, keepdims=True)
 
-        def give(source, j):
-            k = source // 2 * members + j
-            device = where_is(source, j)
-            return [remote(osend.at[k], obuf.at[kind, member], o_send, o_recv.at[kind], device),
-                    remote(ssend.at[k], sbuf.at[kind, member], s_send, s_recv.at[kind], device)]
-
-        begin(plane)
-        for k in range(1, classes):
-            begin(peer_plane(k))
-
-        mate_slots(hand_over)
-
-        for k in range(1, classes):
-            for piece in pieces:
-                finish(peer_plane(k), piece)
-                for j in range(piece.start, piece.stop):
-                    for copy in give(peer_plane(k), j):
-                        copy.start()
-
-        finish(plane, everyone)
-        pltpu.make_async_copy(osend.at[me], obuf.at[kind, member], o_recv.at[kind]).start()
-        pltpu.make_async_copy(ssend.at[me], sbuf.at[kind, member], s_recv.at[kind]).start()
-        for i in range(1, members):
-            for copy in give(plane, lax.rem(member + i, members)):
-                copy.start()
-
-        for g in range(classes):
-            pltpu.make_async_copy(sbuf.at[g], sbuf.at[g], s_recv.at[g]).wait()
-            pltpu.make_async_copy(obuf.at[g], obuf.at[g], o_recv.at[g]).wait()
+        def rows_of(members_part):
+            return slice(members_part.start * slice_rows, members_part.stop * slice_rows)
+
+        def prepare(k, members_part):
+            rows = rows_of(members_part)
+            top, total, weights = weigh(k, members_part, len(sure), late_blocks)
+            late_top[rows] = jnp.broadcast_to(top, (weights.shape[0], HEAD_WIDTH))
+            late_total[rows] = jnp.broadcast_to(total, (weights.shape[0], HEAD_WIDTH))
+            late_weights[rows] = weights
+
+        def finish(k, members_part):
+            rows = rows_of(members_part)
+            early = [ref[rows] for ref in (early_top, early_total, early_acc)]
+            late = [late_top[rows], late_total[rows], summed(late_weights[rows], len(sure))]
+            put(k, members_part, *joined([early, late]))
+
+        def give(k, members_part):
+            for j in range(members_part.start, members_part.stop):
+                n = k * members + j
+                device = where_is(2 * k + half, j)
+                to_me = (kind == k) & (member == j)
+
+                @pl.when(to_me)
+                def _():
+                    pltpu.make_async_copy(osend.at[n], obuf.at[kind, member], o_recv).start()
+                    pltpu.make_async_copy(ssend.at[n], sbuf.at[kind, member], s_recv).start()
+
+                @pl.when(jnp.logical_not(to_me))
+                def _():
+                    remote(osend.at[n], obuf.at[kind, member], o_send, o_recv, device).start()
+                    remote(ssend.at[n], sbuf.at[kind, member], s_send, s_recv, device).start()
+
+        begin(0)
+
+        @pl.when(is_second)
+        def _():
+            mate_slots(hand_over(0))
+            mate_slots(hand_over(1))
+
+        pl.when(is_first)(lambda: mate_slots(lambda i, there, e: landed(0, i)))
+
+        prepare(0, everyone)
+
+        pl.when(is_first)(lambda: mate_slots(lambda i, there, e: landed(1, i)))
+
+        for piece in pieces:
+            finish(0, piece)
+            give(0, piece)
+
+        def attend(k):
+            await_queries(k)
+            put(k, everyone, *part_of(k, everyone, 0, own_blocks + late_blocks))
+            give(k, everyone)
+
+        if classes <= 4:
+            for k in range(1, classes):
+                attend(k)
+        else:
+            pl.loop(1, classes)(attend)
+
+        @pl.when(i_am_live)
+        def _():
+            sent = kvbuf.at[:, pl.ds(0, chips + 1)]
+            pltpu.make_async_copy(sent, sent, kv_send).wait()
+
+        def handed_on(i, there, e):
+            @pl.when(is_second & (chip != e // 2))
+            def _():
+                sent = kvbuf.at[:, pl.ds(0, 2)]
+                pltpu.make_async_copy(sent, sent, pass_send.at[i]).wait()
+
+        def handed_over(i, there, e):
+            sent = kvbuf.at[:, i]
+            pl.when(is_second)(pltpu.make_async_copy(sent, sent, pass_send.at[i]).wait)
+
+        own_slots(handed_on)
+        mate_slots(handed_over)
+        for buffer, sem in ((qbuf, q_send), (osend, o_send), (ssend, s_send)):
+            others = buffer.at[pl.ds(0, messages - 1)]
+            pltpu.make_async_copy(others, others, sem).wait()
+
+        pltpu.make_async_copy(sbuf, sbuf, s_recv).wait()
+        pltpu.make_async_copy(obuf, obuf, o_recv).wait()
 
         for e in range(members):
             column = lambda g, place: jnp.sum(jnp.where(place, sbuf[g, e], 0.0), axis=1, keepdims=True)
@@ -330,45 +421,29 @@
                 first = (e * heads + h) * HEAD_WIDTH
                 out_ref[:, first:first + HEAD_WIDTH] = wide[e, h * local_rows:(h + 1) * local_rows].astype(out_ref.dtype)
 
-        @pl.when(i_am_live)
-        def _():
-            to_partner.wait_send()
-            for k in range(1, chips):
-                kv_copy(k).wait_send()
-            to_mate.wait_send()
-
-        def own_sent(i, there, e):
-            @pl.when(is_second & (chip != e // 2))
-            def _():
-                to_next(i, there).wait_send()
-                to_first(i).wait_send()
-
-        own_slots(own_sent)
-        mate_slots(lambda i, there, e: pl.when(is_second)(to_first(i).wait_send))
-        for buffer, sem in ((qbuf, q_send), (osend, o_send), (ssend, s_send)):
-            others = buffer.at[pl.ds(0, messages - 1)]
-            pltpu.make_async_copy(others, others, sem).wait()
-
     bf16, dma = jnp.bfloat16, pltpu.SemaphoreType.DMA
     signal = pltpu.SemaphoreType.REGULAR
     scratch = [
         pltpu.SMEM((blocks_n,), jnp.int32),
         pltpu.VMEM((local_rows, QUERY_HEADS * HEAD_WIDTH), bf16),
         pltpu.VMEM((2, BLOCK, KEY_VALUE_HEADS * HEAD_WIDTH), bf16),
-        dma((3,)), signal, signal,
+        signal, signal,
         pltpu.VMEM((members, slice_rows, HEAD_WIDTH), bf16),
         pltpu.VMEM((members, slice_rows, HEAD_WIDTH), jnp.float32),
         pltpu.VMEM((messages, slice_rows, HEAD_WIDTH), bf16),
         pltpu.VMEM((2, slots_n, BLOCK, HEAD_WIDTH), bf16),
-        pltpu.VMEM((classes, chunk_rows, HEAD_WIDTH), jnp.float32),
-        pltpu.VMEM((classes, chunk_rows, HEAD_WIDTH), jnp.float32),
-        pltpu.VMEM((classes, chunk_rows, HEAD_WIDTH), jnp.float32),
+        pltpu.VMEM((chunk_rows, HEAD_WIDTH), jnp.float32),
+        pltpu.VMEM((chunk_rows, HEAD_WIDTH), jnp.float32),
+        pltpu.VMEM((chunk_rows, HEAD_WIDTH), jnp.float32),
+        pltpu.VMEM((chunk_rows, HEAD_WIDTH), jnp.float32),
+        pltpu.VMEM((chunk_rows, HEAD_WIDTH), jnp.float32),
+        pltpu.VMEM((chunk_rows, (slots_n - len(sure)) * BLOCK), bf16),
         pltpu.VMEM((messages, slice_rows, HEAD_WIDTH), bf16),
         pltpu.VMEM((messages, 1, BLOCK), jnp.float32),
         pltpu.VMEM((classes, members, slice_rows, HEAD_WIDTH), bf16),
         pltpu.VMEM((classes, members, 1, BLOCK), jnp.float32),
-        dma, dma((classes,)), dma((chips + 1,)), dma((slots_n,)), dma((slots_n,)), dma((slots_n,)),
-        dma, dma((classes,)), dma, dma((classes,)),
+        dma, dma((classes,)), dma, dma((2, slots_n)), dma((slots_n,)),
+        dma, dma, dma, dma,
     ]
     return kernel, scratch
 

time: 20.8 us -> 19.6 us (0.942)
  Pallas kernels: 20.1 us -> 18.8 us
    pallas_call x1, Pallas kernels: 20.1 us -> 18.8 us  [per_device(): pl.pallas_call(kernel, out_shape=pltpu.VMEM(queries.shape, queries.dtype)...]
where the time goes in v4:
time: 19.6 us; the launch traced here: 19.4 us
  Pallas kernels  18.8 us (96%)
  local copies, waits for them, and re-layouts  0.63 us (3%)
    pallas_call x1, Pallas kernels, per_device(): pl.pallas_call(kernel, out_shape=pltpu.VMEM(queries.shape, queries.dtype)...  18.8 us
    unnamed x1, local copies, waits for them, and re-layouts  0.63 us

profile of v4, /device:TPU:0, one launch (start us, length us, event | category | flops | bytes accessed | tf_op | source)
XLA Modules:
  0.0 19.4 jit_solution(5251203963732888801)
XLA Ops:
  0.0 18.8 %shard_map.37 = bf16[4,8192]{1,0:T(4,128)(2,1)S(1)} custom-call(s32[32]{0:T(128)} %doc_any.1, bf16[4,8192]{1,0:T(4,128)(2,1)} %q_any.1, bf16[2,128,512]{2,1,0:T(8,128)(2,1)} %kv_any.1), custom_call_target="tpu_custom_call" | custom-call | tf_op jit(solution)/shard_map/pallas_call | solution.py:457
  18.8 0.6 %copy.5 = bf16[4,8192]{1,0:T(4,128)(2,1)} copy(bf16[4,8192]{1,0:T(4,128)(2,1)S(1)} %shard_map.37) | data formatting | bytes 131072

commit v5 on v4

--- a/solution.py
+++ b/solution.py
@@ -50,6 +50,8 @@
     assert sure and chips & (chips - 1) == 0
     steps = sorted(range(1, chips), key=lambda k: (bin(k).count("1"), -k))
 
+    routes = [steps, steps[::-1]]
+
     def crossed(chip, k):
         bits = [1 << n for n in range(chips.bit_length() - 1) if k >> n & 1]
         return chip + sum(bit * (1 - 2 * (chip // bit % 2)) for bit in bits)
@@ -72,8 +74,9 @@
         mate_core = where_is(mate, chip * 2 + 1)
         is_first, is_second = core == 0, core == 1
         barrier = pltpu.get_barrier_semaphore()
-        fetch = pltpu.make_async_copy(kv_any, local, kv_send)
-        fetch.start()
+        fetches = [pltpu.make_async_copy(kv_any.at[t], local.at[t], sem) for t, sem in enumerate((kv_send, s_send))]
+        for fetch in fetches:
+            fetch.start()
 
         def peer_plane(k):
             return lax.rem(kind + k, classes) * 2 + half
@@ -136,13 +139,19 @@
 
         i_am_live = my_block >= first_live
 
-        fetch.wait()
+        fetches[0].wait()
 
         @pl.when(i_am_live)
         def _():
-            for t in range(2):
-                for k in steps:
-                    kv_copy(t, k).start()
+            for k in routes[0]:
+                kv_copy(0, k).start()
+
+        fetches[1].wait()
+
+        @pl.when(i_am_live)
+        def _():
+            for k in routes[1]:
+                kv_copy(1, k).start()
             for t in range(2):
                 pltpu.make_async_copy(kv_part(t, chip), kvbuf.at[t, my_slot], kv_recv.at[t, my_slot]).start()
                 to_partner(t).start()
@@ -170,8 +179,10 @@
         near = [n for n in range(chips) if n % 2 == 0]
         far = [n for n in range(chips) if n % 2 == 1]
 
+        keys_first = (is_sure == 1) & (kind > 0)
+
         def q_far():
-            for k in range(classes):
+            for k in [*range(1, classes), 0]:
                 q_to(k, far)
 
         pltpu.make_async_copy(qsend.at[member], qbuf.at[me], q_recv.at[kind]).start()
@@ -193,7 +204,7 @@
 
         for k in range(1, classes):
             q_to(k, near)
-        q_far()
+        pl.when(jnp.logical_not(keys_first))(q_far)
 
         def landed(t, i):
             pltpu.make_async_copy(kvbuf.at[t, i], kvbuf.at[t, i], kv_recv.at[t, i]).wait()
@@ -204,23 +215,29 @@
         def to_next(t, i, there):
             return remote(kvbuf.at[t, i], kvbuf.at[t, there], pass_send.at[i], kv_recv.at[t, there], mate_core)
 
-        def in_order(of_half, first, step):
-            for k in [0] + steps:
+        def in_order(of_half, first, step, t=0):
+            def unsure(k):
+                for n, (h, f) in enumerate(maybe):
+                    is_live = (crossed(chip, k) == f // 2) & (of_half == h) & (block_of(f, 2 * kind + h) >= first_live)
+                    pl.when(is_live)(lambda: step(spare + n, spare + n, f))
+
+            if t == 1:
+                for k in [0] + steps:
+                    unsure(k)
+            for k in [0] + routes[t]:
                 for c in (1, 0):
                     e = crossed(chip, k) * 2 + c
                     i = sum(n * (e == f).astype(jnp.int32) for n, f in enumerate(sure))
                     found = sum((e == f).astype(jnp.int32) for f in sure) == 1
                     pl.when(found)(lambda: step(first + i, len(sure) + i, e))
-                    for n, (h, f) in enumerate(maybe):
-                        if f % 2 == c:
-                            is_live = (e == f) & (of_half == h) & (block_of(f, 2 * kind + h) >= first_live)
-                            pl.when(is_live)(lambda: step(spare + n, spare + n, f))
-
-        def own_slots(step):
-            in_order(half, 0, step)
-
-        def mate_slots(step):
-            in_order(1 - half, len(sure), step)
+                if t == 0:
+                    unsure(k)
+
+        def own_slots(step, t=0):
+            in_order(half, 0, step, t)
+
+        def mate_slots(step, t=0):
+            in_order(1 - half, len(sure), step, t)
 
         def hand_on(t):
             def step(i, there, e):
@@ -239,14 +256,16 @@
             return step
 
         own_slots(hand_on(0))
-        own_slots(hand_on(1))
+        pl.when(keys_first)(q_far)
+        own_slots(hand_on(1), 1)
 
         lane = lax.broadcasted_iota(jnp.int32, (chunk_rows, BLOCK), 1)
         row_index = lax.broadcasted_iota(jnp.int32, (chunk_rows, BLOCK), 0)
         row_query = row_index // slice_rows * local_rows + row_index % local_rows
-        offset = (lax.broadcasted_iota(jnp.int32, (slice_rows, BLOCK), 1)
-                  - lax.broadcasted_iota(jnp.int32, (slice_rows, BLOCK), 0))
-        top_place, total_place = offset == 0, offset == slice_rows
+        place = (lax.broadcasted_iota(jnp.int32, (slice_rows, BLOCK), 1)
+                 == lax.broadcasted_iota(jnp.int32, (slice_rows, BLOCK), 0))
+        as_row = lambda column: jnp.sum(jnp.where(place, column, 0.0), axis=0, keepdims=True)
+        as_column = lambda row: jnp.sum(jnp.where(place, row, 0.0), axis=1, keepdims=True)
 
         def weigh(k, members_part, first_slot, blocks):
             first, count = k * members + members_part.start, members_part.stop - members_part.start
@@ -316,8 +335,7 @@
             osend[pl.ds(first, count)] = acc.astype(jnp.bfloat16).reshape(count, slice_rows, HEAD_WIDTH)
             for j in range(count):
                 part = slice(j * slice_rows, (j + 1) * slice_rows)
-                stats = jnp.where(top_place, top[part], jnp.where(total_place, total[part], 0.0))
-                ssend[first + j] = jnp.sum(stats, axis=0, keepdims=True)
+                ssend[first + j] = jnp.concatenate([as_row(top[part]), as_row(total[part])], axis=0)
 
         def rows_of(members_part):
             return slice(members_part.start * slice_rows, members_part.stop * slice_rows)
@@ -348,21 +366,21 @@
 
                 @pl.when(jnp.logical_not(to_me))
                 def _():
+                    remote(ssend.at[n], sbuf.at[kind, member], s_send, s_recv, device).start()
                     remote(osend.at[n], obuf.at[kind, member], o_send, o_recv, device).start()
-                    remote(ssend.at[n], sbuf.at[kind, member], s_send, s_recv, device).start()
 
         begin(0)
 
-        @pl.when(is_second)
-        def _():
-            mate_slots(hand_over(0))
-            mate_slots(hand_over(1))
-
-        pl.when(is_first)(lambda: mate_slots(lambda i, there, e: landed(0, i)))
+        def wait_only(t):
+            return lambda i, there, e: landed(t, i)
+
+        pl.when(is_second)(lambda: mate_slots(hand_over(0)))
+        pl.when(is_first)(lambda: mate_slots(wait_only(0)))
 
         prepare(0, everyone)
 
-        pl.when(is_first)(lambda: mate_slots(lambda i, there, e: landed(1, i)))
+        pl.when(is_second)(lambda: mate_slots(hand_over(1), 1))
+        pl.when(is_first)(lambda: mate_slots(wait_only(1), 1))
 
         for piece in pieces:
             finish(0, piece)
@@ -401,22 +419,21 @@
             pltpu.make_async_copy(others, others, sem).wait()
 
         pltpu.make_async_copy(sbuf, sbuf, s_recv).wait()
-        pltpu.make_async_copy(obuf, obuf, o_recv).wait()
-
+        shares = []
         for e in range(members):
-            column = lambda g, place: jnp.sum(jnp.where(place, sbuf[g, e], 0.0), axis=1, keepdims=True)
-            tops = [column(g, top_place) for g in range(classes)]
+            tops = [sbuf[g, e, 0:1] for g in range(classes)]
             overall = tops[0]
             for t in tops[1:]:
                 overall = jnp.maximum(overall, t)
-            merged = weight = None
-            for g in range(classes):
-                factor = jnp.exp2((tops[g] - overall) * scale)
-                term = factor * obuf[g, e].astype(jnp.float32)
-                part = factor * column(g, total_place)
-                merged = term if merged is None else merged + term
-                weight = part if weight is None else weight + part
-            wide[e] = merged / weight
+            factors = [jnp.exp2((t - overall) * scale) for t in tops]
+            weight = sum(f * sbuf[g, e, 1:2] for g, f in enumerate(factors))
+            weight = jnp.where(weight > 0.0, weight, 1.0)
+            shares.append([as_column(f / weight) for f in factors])
+
+        pltpu.make_async_copy(obuf, obuf, o_recv).wait()
+
+        for e in range(members):
+            wide[e] = sum(share * obuf[g, e].astype(jnp.float32) for g, share in enumerate(shares[e]))
             for h in range(heads):
                 first = (e * heads + h) * HEAD_WIDTH
                 out_ref[:, first:first + HEAD_WIDTH] = wide[e, h * local_rows:(h + 1) * local_rows].astype(out_ref.dtype)
@@ -439,9 +456,9 @@
         pltpu.VMEM((chunk_rows, HEAD_WIDTH), jnp.float32),
         pltpu.VMEM((chunk_rows, (slots_n - len(sure)) * BLOCK), bf16),
         pltpu.VMEM((messages, slice_rows, HEAD_WIDTH), bf16),
-        pltpu.VMEM((messages, 1, BLOCK), jnp.float32),
+        pltpu.VMEM((messages, 2, BLOCK), jnp.float32),
         pltpu.VMEM((classes, members, slice_rows, HEAD_WIDTH), bf16),
-        pltpu.VMEM((classes, members, 1, BLOCK), jnp.float32),
+        pltpu.VMEM((classes, members, 2, BLOCK), jnp.float32),
         dma, dma((classes,)), dma, dma((2, slots_n)), dma((slots_n,)),
         dma, dma, dma, dma,
     ]

time: 19.6 us -> 19.3 us (0.985)
  Pallas kernels: 18.8 us -> 18.5 us
    pallas_call x1, Pallas kernels: 18.8 us -> 18.5 us  [per_device(): pl.pallas_call(kernel, out_shape=pltpu.VMEM(queries.shape, queries.dtype)...]
where the time goes in v5:
time: 19.3 us; the launch traced here: 19.2 us
  Pallas kernels  18.5 us (96%)
  local copies, waits for them, and re-layouts  0.63 us (3%)
    pallas_call x1, Pallas kernels, per_device(): pl.pallas_call(kernel, out_shape=pltpu.VMEM(queries.shape, queries.dtype)...  18.5 us
    unnamed x1, local copies, waits for them, and re-layouts  0.63 us

profile of v5, /device:TPU:0, one launch (start us, length us, event | category | flops | bytes accessed | tf_op | source)
XLA Modules:
  0.0 19.2 jit_solution(10261489344476688983)
XLA Ops:
  0.0 18.5 %shard_map.37 = bf16[4,8192]{1,0:T(4,128)(2,1)S(1)} custom-call(s32[32]{0:T(128)} %doc_any.1, bf16[4,8192]{1,0:T(4,128)(2,1)} %q_any.1, bf16[2,128,512]{2,1,0:T(8,128)(2,1)} %kv_any.1), custom_call_target="tpu_custom_call" | custom-call | tf_op jit(solution)/shard_map/pallas_call | solution.py:474
  18.5 0.6 %copy.5 = bf16[4,8192]{1,0:T(4,128)(2,1)} copy(bf16[4,8192]{1,0:T(4,128)(2,1)S(1)} %shard_map.37) | data formatting | bytes 131072

commit v6 on v5

--- a/solution.py
+++ b/solution.py
@@ -261,7 +261,7 @@
 
         lane = lax.broadcasted_iota(jnp.int32, (chunk_rows, BLOCK), 1)
         row_index = lax.broadcasted_iota(jnp.int32, (chunk_rows, BLOCK), 0)
-        row_query = row_index // slice_rows * local_rows + row_index % local_rows
+        key_ahead = lane - (row_index // slice_rows * local_rows + row_index % local_rows)
         place = (lax.broadcasted_iota(jnp.int32, (slice_rows, BLOCK), 1)
                  == lax.broadcasted_iota(jnp.int32, (slice_rows, BLOCK), 0))
         as_row = lambda column: jnp.sum(jnp.where(place, column, 0.0), axis=0, keepdims=True)
@@ -273,7 +273,7 @@
             q = qbuf[pl.ds(first, count)].reshape(count * slice_rows, HEAD_WIDTH)
             query_first = (2 * k + half) * chunk_queries
             query_block = (query_first // BLOCK + 1) * stripe_blocks - 1
-            in_block = row_query[rows] + query_first % BLOCK
+            ahead = key_ahead[rows] - query_first % BLOCK
             query_doc = doc_ref[query_block]
             held = slice(first_slot, first_slot + len(blocks))
             keys = kvbuf[0, held].reshape(len(blocks) * BLOCK, HEAD_WIDTH)
@@ -281,10 +281,9 @@
             masked = []
             for i, b in enumerate(blocks):
                 same = doc_ref[b] == query_doc
-                whole = jnp.where(same & (b < query_block), BLOCK, -1)
-                causal = jnp.where(same & (b == query_block), 0, -2 * BLOCK)
-                limit = jnp.maximum(in_block + causal, whole)
-                masked.append(jnp.where(lane[rows] <= limit, scores[:, i * BLOCK:(i + 1) * BLOCK], masked_score))
+                reach = jnp.where(b < query_block, BLOCK, jnp.where(b == query_block, 0, -2 * BLOCK))
+                reach = jnp.where(same, reach, -2 * BLOCK)
+                masked.append(jnp.where(ahead <= reach, scores[:, i * BLOCK:(i + 1) * BLOCK], masked_score))
             top = masked[0]
             for s in masked[1:]:
                 top = jnp.maximum(top, s)
@@ -361,13 +360,13 @@
 
                 @pl.when(to_me)
                 def _():
-                    pltpu.make_async_copy(osend.at[n], obuf.at[kind, member], o_recv).start()
-                    pltpu.make_async_copy(ssend.at[n], sbuf.at[kind, member], s_recv).start()
+                    pltpu.make_async_copy(osend.at[n], obuf.at[core, kind, chip], o_recv.at[core]).start()
+                    pltpu.make_async_copy(ssend.at[n], sbuf.at[core, kind, chip], s_recv.at[core]).start()
 
                 @pl.when(jnp.logical_not(to_me))
                 def _():
-                    remote(ssend.at[n], sbuf.at[kind, member], s_send, s_recv, device).start()
-                    remote(osend.at[n], obuf.at[kind, member], o_send, o_recv, device).start()
+                    remote(ssend.at[n], sbuf.at[core, kind, chip], s_send, s_recv.at[core], device).start()
+                    remote(osend.at[n], obuf.at[core, kind, chip], o_send, o_recv.at[core], device).start()
 
         begin(0)
 
@@ -418,25 +417,28 @@
             others = buffer.at[pl.ds(0, messages - 1)]
             pltpu.make_async_copy(others, others, sem).wait()
 
-        pltpu.make_async_copy(sbuf, sbuf, s_recv).wait()
-        shares = []
-        for e in range(members):
-            tops = [sbuf[g, e, 0:1] for g in range(classes)]
-            overall = tops[0]
-            for t in tops[1:]:
-                overall = jnp.maximum(overall, t)
-            factors = [jnp.exp2((t - overall) * scale) for t in tops]
-            weight = sum(f * sbuf[g, e, 1:2] for g, f in enumerate(factors))
-            weight = jnp.where(weight > 0.0, weight, 1.0)
-            shares.append([as_column(f / weight) for f in factors])
-
-        pltpu.make_async_copy(obuf, obuf, o_recv).wait()
-
-        for e in range(members):
-            wide[e] = sum(share * obuf[g, e].astype(jnp.float32) for g, share in enumerate(shares[e]))
-            for h in range(heads):
-                first = (e * heads + h) * HEAD_WIDTH
-                out_ref[:, first:first + HEAD_WIDTH] = wide[e, h * local_rows:(h + 1) * local_rows].astype(out_ref.dtype)
+        def collect(c):
+            pltpu.make_async_copy(sbuf.at[c], sbuf.at[c], s_recv.at[c]).wait()
+            shares = []
+            for n in range(chips):
+                tops = [sbuf[c, g, n, 0:1] for g in range(classes)]
+                overall = tops[0]
+                for t in tops[1:]:
+                    overall = jnp.maximum(overall, t)
+                factors = [jnp.exp2((t - overall) * scale) for t in tops]
+                weight = sum(f * sbuf[c, g, n, 1:2] for g, f in enumerate(factors))
+                weight = jnp.where(weight > 0.0, weight, 1.0)
+                shares.append([as_column(f / weight) for f in factors])
+            pltpu.make_async_copy(obuf.at[c], obuf.at[c], o_recv.at[c]).wait()
+            for n in range(chips):
+                e = 2 * n + c
+                wide[e] = sum(share * obuf[c, g, n].astype(jnp.float32) for g, share in enumerate(shares[n]))
+                for h in range(heads):
+                    first = (e * heads + h) * HEAD_WIDTH
+                    out_ref[:, first:first + HEAD_WIDTH] = wide[e, h * local_rows:(h + 1) * local_rows].astype(out_ref.dtype)
+
+        collect(1)
+        collect(0)
 
     bf16, dma = jnp.bfloat16, pltpu.SemaphoreType.DMA
     signal = pltpu.SemaphoreType.REGULAR
@@ -457,10 +459,10 @@
         pltpu.VMEM((chunk_rows, (slots_n - len(sure)) * BLOCK), bf16),
         pltpu.VMEM((messages, slice_rows, HEAD_WIDTH), bf16),
         pltpu.VMEM((messages, 2, BLOCK), jnp.float32),
-        pltpu.VMEM((classes, members, slice_rows, HEAD_WIDTH), bf16),
-        pltpu.VMEM((classes, members, 2, BLOCK), jnp.float32),
+        pltpu.VMEM((2, classes, chips, slice_rows, HEAD_WIDTH), bf16),
+        pltpu.VMEM((2, classes, chips, 2, BLOCK), jnp.float32),
         dma, dma((classes,)), dma, dma((2, slots_n)), dma((slots_n,)),
-        dma, dma, dma, dma,
+        dma, dma((2,)), dma, dma((2,)),
     ]
     return kernel, scratch
 

time: 19.3 us -> 19.3 us (level)
  no operation moved by 1% of the time
where the time goes in v6:
time: 19.3 us; the launch traced here: 19.1 us
  Pallas kernels  18.5 us (96%)
  local copies, waits for them, and re-layouts  0.63 us (3%)
    pallas_call x1, Pallas kernels, per_device(): pl.pallas_call(kernel, out_shape=pltpu.VMEM(queries.shape, queries.dtype)...  18.5 us
    unnamed x1, local copies, waits for them, and re-layouts  0.63 us

profile of v6, /device:TPU:0, one launch (start us, length us, event | category | flops | bytes accessed | tf_op | source)
XLA Modules:
  0.0 19.1 jit_solution(5109101721667004449)
XLA Ops:
  0.0 18.5 %shard_map.37 = bf16[4,8192]{1,0:T(4,128)(2,1)S(1)} custom-call(s32[32]{0:T(128)} %doc_any.1, bf16[4,8192]{1,0:T(4,128)(2,1)} %q_any.1, bf16[2,128,512]{2,1,0:T(8,128)(2,1)} %kv_any.1), custom_call_target="tpu_custom_call" | custom-call | tf_op jit(solution)/shard_map/pallas_call | solution.py:476
  18.5 0.6 %copy.5 = bf16[4,8192]{1,0:T(4,128)(2,1)} copy(bf16[4,8192]{1,0:T(4,128)(2,1)S(1)} %shard_map.37) | data formatting | bytes 131072

commit v7 on v6

--- a/solution.py
+++ b/solution.py
@@ -50,7 +50,7 @@
     assert sure and chips & (chips - 1) == 0
     steps = sorted(range(1, chips), key=lambda k: (bin(k).count("1"), -k))
 
-    routes = [steps, steps[::-1]]
+    routes = [steps, [*steps[1:], steps[0]]]
 
     def crossed(chip, k):
         bits = [1 << n for n in range(chips.bit_length() - 1) if k >> n & 1]
@@ -59,7 +59,7 @@
     def where_is(plane, member):
         return (plane * fold + member // cols_n, member % cols_n)
 
-    def kernel(doc_any, q_any, kv_any, out_ref, doc_ref, q_ref, local, plane_sem, cross_sem,
+    def kernel(doc_any, q_any, kv_any, out_ref, doc_ref, q_ref, local, ready_sem,
                qsend, wide, qbuf, kvbuf, early_top, early_total, early_acc, late_top, late_total, late_weights, osend, ssend, obuf, sbuf,
                q_send, q_recv, kv_send, kv_recv, pass_send, o_send, o_recv, s_send, s_recv):
         row, col = lax.axis_index("qrow"), lax.axis_index("kcol")
@@ -105,11 +105,11 @@
         @pl.when(is_second)
         def _():
             pl.semaphore_wait(barrier, members - 1)
-            pl.semaphore_signal(plane_sem, inc=1, device_id=partner, device_id_type=MESH)
+            pl.semaphore_signal(ready_sem, inc=1, device_id=partner, device_id_type=MESH)
 
         @pl.when(is_first)
         def _():
-            pl.semaphore_wait(plane_sem, 1)
+            pl.semaphore_wait(ready_sem, 1)
 
         def remote(src, dst, sent, got, device):
             return pltpu.make_async_remote_copy(
@@ -191,11 +191,11 @@
         @pl.when(is_first)
         def _():
             pl.semaphore_wait(barrier, (classes - 1) * members + 2)
-            pl.semaphore_signal(cross_sem, inc=1, device_id=partner, device_id_type=MESH)
+            pl.semaphore_signal(ready_sem, inc=1, device_id=partner, device_id_type=MESH)
 
         @pl.when(is_second)
         def _():
-            pl.semaphore_wait(cross_sem, 1)
+            pl.semaphore_wait(ready_sem, 1)
 
         @pl.when(i_am_live)
         def _():
@@ -446,7 +446,7 @@
         pltpu.SMEM((blocks_n,), jnp.int32),
         pltpu.VMEM((local_rows, QUERY_HEADS * HEAD_WIDTH), bf16),
         pltpu.VMEM((2, BLOCK, KEY_VALUE_HEADS * HEAD_WIDTH), bf16),
-        signal, signal,
+        signal,
         pltpu.VMEM((members, slice_rows, HEAD_WIDTH), bf16),
         pltpu.VMEM((members, slice_rows, HEAD_WIDTH), jnp.float32),
         pltpu.VMEM((messages, slice_rows, HEAD_WIDTH), bf16),

time: 19.3 us -> 19.3 us (level)
  no operation moved by 1% of the time
where the time goes in v7:
time: 19.3 us; the launch traced here: 19.1 us
  Pallas kernels  18.5 us (96%)
  local copies, waits for them, and re-layouts  0.63 us (3%)
    pallas_call x1, Pallas kernels, per_device(): pl.pallas_call(kernel, out_shape=pltpu.VMEM(queries.shape, queries.dtype)...  18.5 us
    unnamed x1, local copies, waits for them, and re-layouts  0.63 us

profile of v7, /device:TPU:0, one launch (start us, length us, event | category | flops | bytes accessed | tf_op | source)
XLA Modules:
  0.0 19.1 jit_solution(10626734748001407842)
XLA Ops:
  0.0 18.5 %shard_map.37 = bf16[4,8192]{1,0:T(4,128)(2,1)S(1)} custom-call(s32[32]{0:T(128)} %doc_any.1, bf16[4,8192]{1,0:T(4,128)(2,1)} %q_any.1, bf16[2,128,512]{2,1,0:T(8,128)(2,1)} %kv_any.1), custom_call_target="tpu_custom_call" | custom-call | tf_op jit(solution)/shard_map/pallas_call | solution.py:476
  18.5 0.6 %copy.5 = bf16[4,8192]{1,0:T(4,128)(2,1)} copy(bf16[4,8192]{1,0:T(4,128)(2,1)S(1)} %shard_map.37) | data formatting | bytes 131072
